TPU v7x, 32 devices: a whole 2x2x4 slice. The times are simulated.
32 devices in a mesh: groups: 2 (over x), inst: 4 (over z), tp: 4 (over y, core).
Axes of the slice: x: 2, y: 2, z: 4, core: 2. Of those that a mesh axis runs over, the one named last changes fastest.
Arguments:
- qkv_first: bfloat16 [48, 10240], P(('groups', 'inst'), 'tp'), parts along dimension 0, may hold values from -5 to 5
- qkv_second: bfloat16 [48, 10240], P(('groups', 'inst'), 'tp'), parts along dimension 0, may hold values from -5 to 5
- w_out: bfloat16 [8192, 8192], P(None, 'tp'), may hold values from -0.5 to 0.5
- kv_cache: bfloat16 [512, 2, 16, 1024], P(('groups', 'inst', 'tp')), parts along dimension 0, may hold values from -4096 to 4096
- lengths: int32 [48], P('groups'), parts along dimension 0, may hold values from 4 to 126, as said below
- page_table: int32 [48, 8], P(('groups', 'inst')), parts along dimension 0, may hold values from -1 to 63, as said below
- moves: int32 [8, 2], P('groups'), parts along dimension 0, may hold values from 0 to 23, as said below
- dest_pages: int32 [8, 8], P('groups'), parts along dimension 0, may hold values from 0 to 63, as said below
Outputs:
- out_first: bfloat16 [48, 8192], P(('groups', 'inst'), 'tp'), parts along dimension 0
- out_second: bfloat16 [48, 8192], P(('groups', 'inst'), 'tp'), parts along dimension 0
- kv_out: bfloat16 [512, 2, 16, 1024], P(('groups', 'inst', 'tp')), parts along dimension 0
There are 2 independent parts, one for each index of `groups`. A program takes and returns all parts, laid end to end along the dimension named above; an argument that names none is the same for every part. Nothing has to cross between parts.
Inputs may be any that keep to these rules, and one draw needn't show every extreme that they name: Half of the instances, drawn afresh, are heavy: lengths of their requests run from 64 to 126, those of the other instances from 4 to 16. Entry j of request r is a page of its instance's pool for j < ceil((lengths[r] + 2) / 16) and -1 after; such a page p has floor(p / 16) = j mod (4); no pool page is named twice by page_table and dest_pages together. Row i moves request moves[i, 0], a number from 0 to 23, to instance moves[i, 1], a number from 0 to 3; every heavy instance sends exactly one request to every other instance, those are the light ones, and a moved request's length is at least (7) * 16 - 1. `dest_pages`: entry j of row i, for every j < 8, is a page p of the destination's pool that page_table leaves free, with floor(p / 16) = j mod (4).
All inputs are finite; a program needn't handle non-finite values.
Results may differ from a plain program's by a relative error of at most 0.015.
Values may be sent and summed in bfloat16 or wider, within the bound.
A program may use at most 64 MiB of HBM per device.

v0:
```python
import math

import jax
import jax.numpy as jnp
from jax import lax
from jax.sharding import PartitionSpec as P

QUERY_HEADS = 64
KEY_VALUE_HEADS = 8
HEAD_SIZE = 128


NEG_LARGE = -1e30


def merged(x, axis, combine):
    everything = jax.tree.map(lambda part: lax.all_gather(part, axis), x)
    initial = jax.tree.map(lambda part: part[0], everything)

    def step(k, so_far):
        return combine(so_far, jax.tree.map(lambda part: part[k], everything))

    return lax.fori_loop(1, lax.axis_size(axis), step, initial)


def gather_rows(token_rows):
    return lax.all_gather(token_rows, "tp", axis=1, tiled=True)


def ownership(index_table, tp_rank, shared_pages):
    page_ids = tp_rank * shared_pages + jnp.arange(shared_pages, dtype=jnp.int32)
    matches = index_table[None, :, :] == page_ids[:, None, None]
    owner_int = jnp.any(matches, axis=2).astype(jnp.int32)
    slot_ids = jnp.arange(index_table.shape[1], dtype=jnp.int32)
    page_number = jnp.sum(jnp.where(matches, slot_ids[None, None, :], 0), axis=(1, 2))
    page_owned = jnp.sum(owner_int, axis=1) > 0
    return (owner_int, page_number, page_owned)


def write_tokens(paged_memory, owners, positions, full_rows):
    owner_int, page_number, page_owned = owners
    shared_pages = paged_memory.shape[0]
    page_extent = paged_memory.shape[2]
    key_value_width = paged_memory.shape[3]
    kv_start = QUERY_HEADS * HEAD_SIZE
    fresh = full_rows[:, kv_start : kv_start + 2 * key_value_width]
    placed = jnp.dot(
        owner_int.astype(jnp.bfloat16), fresh, preferred_element_type=jnp.float32
    ).astype(jnp.bfloat16)
    placed = placed.reshape(shared_pages, 2, 1, key_value_width)
    page_target = jnp.sum(owner_int * positions[None, :], axis=1)
    offsets = page_number[:, None] * page_extent + jnp.arange(page_extent, dtype=jnp.int32)[None, :]
    page_hit = page_owned[:, None] & (offsets == page_target[:, None])
    return jnp.where(page_hit[:, None, :, None], placed, paged_memory)


def partials(paged_memory, owners, counts, full_rows):
    owner_int, page_number, page_owned = owners
    shared_pages = paged_memory.shape[0]
    page_extent = paged_memory.shape[2]
    group_width = QUERY_HEADS // KEY_VALUE_HEADS
    query_per_page = jnp.dot(
        owner_int.astype(jnp.bfloat16),
        full_rows[:, : QUERY_HEADS * HEAD_SIZE],
        preferred_element_type=jnp.float32,
    ).astype(jnp.bfloat16)
    heads_of_query = query_per_page.reshape(shared_pages, KEY_VALUE_HEADS, group_width, HEAD_SIZE)
    gathered_keys = paged_memory[:, 0].reshape(
        shared_pages, page_extent, KEY_VALUE_HEADS, HEAD_SIZE
    )
    gathered_values = paged_memory[:, 1].reshape(
        shared_pages, page_extent, KEY_VALUE_HEADS, HEAD_SIZE
    )
    logit_scores = jnp.einsum(
        "pkgd,ptkd->pkgt", heads_of_query, gathered_keys, preferred_element_type=jnp.float32
    ) / math.sqrt(HEAD_SIZE)
    page_count = jnp.sum(owner_int * counts[None, :], axis=1)
    offsets = page_number[:, None] * page_extent + jnp.arange(page_extent, dtype=jnp.int32)[None, :]
    visible = page_owned[:, None] & (offsets < page_count[:, None])
    position_mask = visible[:, None, None, :]
    logit_scores = jnp.where(position_mask, logit_scores, NEG_LARGE)
    page_top = jnp.max(logit_scores, axis=3).reshape(shared_pages, QUERY_HEADS)
    owner_mask = owner_int[:, :, None] > 0
    row_top = jnp.max(jnp.where(owner_mask, page_top[:, None, :], NEG_LARGE), axis=0)
    page_pointer = jnp.max(jnp.where(owner_mask, row_top[None, :, :], NEG_LARGE), axis=1)
    exponent = jnp.where(
        position_mask,
        jnp.exp(logit_scores - page_pointer.reshape(shared_pages, KEY_VALUE_HEADS, group_width, 1)),
        0.0,
    )
    page_total = jnp.sum(exponent, axis=3).reshape(shared_pages, QUERY_HEADS)
    weights = exponent.astype(jnp.bfloat16)
    page_sums = jnp.einsum(
        "pkgt,ptkd->pkgd", weights, gathered_values, preferred_element_type=jnp.float32
    ).reshape(shared_pages, QUERY_HEADS * HEAD_SIZE)
    owner_float = owner_int.astype(jnp.float32)
    totals = jnp.einsum("pr,ph->rh", owner_float, page_total, precision=lax.Precision.HIGHEST)
    accumulated = jnp.einsum("pr,ph->rh", owner_float, page_sums, precision=lax.Precision.HIGHEST)
    return (row_top, totals, accumulated)


def join_parts(former, latter):
    top_former, total_former, summed_former = former
    top_latter, total_latter, summed_latter = latter
    row_top = jnp.maximum(top_former, top_latter)
    scale_former = jnp.exp(top_former - row_top)
    scale_latter = jnp.exp(top_latter - row_top)
    row_total = total_former * scale_former + total_latter * scale_latter
    row_count = summed_former.shape[0]
    joined = (
        summed_former.reshape(row_count, -1, HEAD_SIZE) * scale_former[:, :, None]
        + summed_latter.reshape(row_count, -1, HEAD_SIZE) * scale_latter[:, :, None]
    )
    return (row_top, row_total, joined.reshape(row_count, -1))


def safe_total(row_total):
    return jnp.where(row_total > 0.0, row_total, 1.0)


def mixed_heads(parts):
    maxima, totals, accumulated = parts
    row_top, row_total, summed = merged((maxima, totals, accumulated), "tp", join_parts)
    row_count = summed.shape[0]
    return (
        (summed.reshape(row_count, -1, HEAD_SIZE) / safe_total(row_total)[..., None])
        .reshape(row_count, -1)
        .astype(jnp.bfloat16)
    )


def project(mixed, w_out):
    return jnp.dot(mixed, w_out, preferred_element_type=jnp.float32).astype(jnp.bfloat16)


def local(qkv_first, qkv_second, w_out, kv_cache, lengths, page_table, moves, dest_pages):
    tp_count = lax.axis_size("tp")
    inst_count = lax.axis_size("inst")
    tp_rank = lax.axis_index("tp")
    inst_index = lax.axis_index("inst")
    row_count = page_table.shape[0]
    shared_pages = kv_cache.shape[0]
    max_pages = page_table.shape[1]
    per_rank = max_pages // tp_count
    my_lengths = lax.dynamic_slice_in_dim(lengths, inst_index * row_count, row_count)
    first_full = gather_rows(qkv_first)
    owners_one = ownership(page_table, tp_rank, shared_pages)
    cache_one = write_tokens(kv_cache, owners_one, my_lengths, first_full)
    out_first = project(
        mixed_heads(partials(cache_one, owners_one, my_lengths + 1, first_full)), w_out
    )
    move_request = moves[:, 0]
    move_dest = moves[:, 1]
    move_source = move_request // row_count
    instances = jnp.arange(inst_count, dtype=jnp.int32)
    move_ids = jnp.arange(moves.shape[0], dtype=jnp.int32)
    send_match = (move_source[None, :] == inst_index) & (move_dest[None, :] == instances[:, None])
    send_has = jnp.any(send_match, axis=1)
    send_move = jnp.sum(jnp.where(send_match, move_ids[None, :], 0), axis=1)
    send_rows = jnp.where(send_has, move_request[send_move] - inst_index * row_count, 0)
    rank_cols = tp_rank + tp_count * jnp.arange(per_rank, dtype=jnp.int32)
    send_pages = jnp.clip(
        page_table[send_rows][:, rank_cols] - tp_rank * shared_pages, 0, shared_pages - 1
    )
    recv_match = (move_source[None, :] == instances[:, None]) & (move_dest[None, :] == inst_index)
    recv_has = jnp.any(recv_match, axis=1)
    recv_move = jnp.sum(jnp.where(recv_match, move_ids[None, :], 0), axis=1)
    recv_table = jnp.where(recv_has[:, None], dest_pages[recv_move], -1)
    recv_pages = recv_table[:, rank_cols] - tp_rank * shared_pages
    second_full = gather_rows(qkv_second)
    positions = my_lengths + 1
    cache_pre = write_tokens(cache_one, owners_one, positions, second_full)
    out_second = project(
        mixed_heads(partials(cache_pre, owners_one, positions + 1, second_full)), w_out
    )
    paged_memory = cache_pre
    outgoing = jnp.where(
        send_has[:, None, None, None, None], paged_memory[send_pages], jnp.zeros((), jnp.bfloat16)
    )
    arrived = lax.all_to_all(outgoing, "inst", split_axis=0, concat_axis=0, tiled=True)
    targets = jnp.where(recv_has[:, None], recv_pages, shared_pages).reshape(-1)
    paged_memory = paged_memory.at[targets].set(
        arrived.reshape((-1,) + paged_memory.shape[1:]), mode="drop"
    )
    freed_rows = jnp.where(send_has[:, None], send_pages, shared_pages).reshape(-1)
    cleared = jnp.zeros((freed_rows.shape[0],) + paged_memory.shape[1:], jnp.bfloat16)
    kv_out = paged_memory.at[freed_rows].set(cleared, mode="drop")
    return (out_first, out_second, kv_out)


def solution(mesh):
    placed = (
        P(("groups", "inst"), "tp"),
        P(("groups", "inst"), "tp"),
        P(None, "tp"),
        P(("groups", "inst", "tp"), None, None, None),
        P("groups"),
        P(("groups", "inst"), None),
        P("groups", None),
        P("groups", None),
    )
    return jax.shard_map(
        local,
        mesh=mesh,
        in_specs=placed,
        out_specs=(
            P(("groups", "inst"), "tp"),
            P(("groups", "inst"), "tp"),
            P(("groups", "inst", "tp"), None, None, None),
        ),
        check_vma=False,
    )
```

profile of v0, /device:TPU:0, one launch (start us, length us, event | category | flops | bytes accessed | tf_op | source)
XLA Modules:
  0.0 124.2 jit_solution(9361369197054579896)
XLA Ops:
  0.7 0.8 compare_reduce_fusion
  1.4 0.8 fusion.42
  2.2 0.8 slice_bitcast_fusion.7
  3.0 0.8 broadcast_compare_fusion
  4.0 0.7 broadcast_add_fusion.1
  4.9 6.9 %all_gather.42 = bf16[6,10240]{1,0:T(8,128)(2,1)S(1)} all-gather(bf16[6,2560]{1,0:T(8,128)(2,1)} %param.12), channel_id=1, replica_groups=mesh['groups'=2,'inst'=4,'tp'=4] {'tp'}, dimensions={1}, use_global_device_ids=true | all-gather | bytes 153600 | tf_op jit(solution)/shard_map/all_gather | solution.py:27
  12.0 5.8 %all_gather.49 = bf16[6,10240]{1,0:T(8,128)(2,1)S(1)} all-gather(bf16[6,2560]{1,0:T(8,128)(2,1)} %param.13), channel_id=1, replica_groups=mesh['groups'=2,'inst'=4,'tp'=4] {'tp'}, dimensions={1}, use_global_device_ids=true | all-gather | bytes 153600 | tf_op jit(solution)/shard_map/all_gather | solution.py:27
  18.1 0.6 gather_fusion.2
  18.8 1.2 %gather_fusion.3 = s32[4,8]{1,0:T(4,128)S(1)} fusion(s32[6,8]{1,0:T(8,128)} %param.17, s32[1024]{0:T(1024)S(1)} %pad_clamp_fusion.1), kind=kCustom, calls=%fused_computation.3 | custom fusion | bytes 272 | tf_op jit(solution)/shard_map/gather | solution.py:163
  20.1 0.6 gather_fusion.4
  21.0 1.5 %broadcast_select_fusion = (bf16[16,2,16,1024]{3,2,1,0:T(8,128)(2,1)S(1)}, bf16[16,2,16,1024]{3,2,1,0:T(8,128)(2,1)S(1)}) fusion(pred[16,16]{1,0:T(8,128)(4,1)S(1)} %get-tuple-element.420, bf16[16,2,1024]{2,1,0:T(2,128)(2,1)S(1)} %broadcast_in_dim.281, bf16[16,2,16,1024]{3,2,1,0:T(8,128)(2,1)} %param.15, bf16[16,2,1024]{2,1,0:T(2,128)(2,1)S(1)} %broadcast_in_dim.270, ...), kind=kLoop, calls=%fused_computation.46 | loop fusion | flops 1048576 | bytes 3277312 | tf_op jit(solution)/shard_map/jit(_where)/select_n | solution.py:54
  22.5 0.6 gather_fusion.5
  23.1 0.9 broadcast_select_fusion.2
  24.0 5.1 %all-to-all-start = ((bf16[4,2,2,16,1024]{4,3,2,1,0:T(8,128)(2,1)}), bf16[4,2,2,16,1024]{4,3,2,1,0:T(8,128)(2,1)}, u32[]{:S(2)}, u32[]{:S(2)}) async-start(bf16[4,2,2,16,1024]{4,3,2,1,0:T(8,128)(2,1)} %broadcast_select_fusion.2), calls=%async_computation | async-start | bytes 1048576 | tf_op jit(solution)/shard_map/all_to_all | solution.py:180
  29.4 1.9 %fusion.9 = bf16[2,8,64,128]{3,1,2,0:T(8,128)(2,1)} fusion(bf16[6,10240]{1,0:T(8,128)(2,1)} %copy-done.2, pred[16,6]{0,1:T(8,128)(4,1)S(1)} %compare_reduce_fusion), kind=kOutput, calls=%fused_computation.43 | convolution fusion | flops 1704128 | bytes 393312 | tf_op jit(solution)/shard_map/dot_general | solution.py:62
  31.3 0.7 fusion.54
  32.0 0.7 select_reduce_fusion.8
  32.7 0.9 fusion.66
  33.7 0.5 fusion.68
  34.5 1.0 copy.74
  35.5 0.5 fusion.67
  36.6 0.3 fusion.14
  36.9 0.7 convolution_bitcast_fusion
  37.6 10.1 %all-gather.11 = f32[4,6,8192]{2,1,0:T(8,128)S(1)} all-gather(f32[1,6,8192]{2,1,0:T(8,128)S(1)} %convolution_bitcast_fusion), channel_id=7, replica_groups=mesh['groups'=2,'inst'=4,'tp'=4] {'tp'}, dimensions={0}, use_global_device_ids=true | all-gather | bytes 983040 | tf_op jit(solution)/shard_map/all_gather | solution.py:17
  47.7 0.7 copy.49
  48.4 0.8 copy.50
  49.2 2.0 %fusion.21 = (f32[16,8,8]{2,1,0:T(8,128)}, f32[16,8,8]{2,1,0:T(8,128)}) fusion(f32[16,8,8,16]{3,2,1,0:T(8,128)S(1)} %get-tuple-element.429, f32[16,8,8]{2,1,0:T(8,128)S(1)} %copy.50, pred[16,16]{1,0:T(8,128)(4,1)} %copy-done.3, f32[16,8,8,16]{3,2,1,0:T(8,128)S(1)} %get-tuple-element.427, f32[16,8,8]{2,1,0:T(8,128)S(1)} %copy.57, pred[16,16]{1,0:T(8,128)(4,1)} %copy-done.4), kind=kLoop, calls=%fused_computation.62 | loop fusion | flops 96256 | bytes 147968 | tf_op jit(solution)/shard_map/reduce_sum | solution.py:91
  51.2 0.9 copy.58
  52.3 5.2 %all-gather.10 = f32[4,6,64]{2,1,0:T(8,128)S(1)} all-gather(f32[1,6,64]{2,1,0:T(8,128)S(1)} %convolution_bitcast_fusion.2), channel_id=6, replica_groups=mesh['groups'=2,'inst'=4,'tp'=4] {'tp'}, dimensions={0}, use_global_device_ids=true | all-gather | bytes 7680 | tf_op jit(solution)/shard_map/all_gather | solution.py:17
  57.5 5.2 %all-gather.9 = f32[4,6,64]{2,1,0:T(8,128)S(1)} all-gather(f32[1,6,64]{2,1,0:T(8,128)S(1)} %bitcast.214), channel_id=5, replica_groups=mesh['groups'=2,'inst'=4,'tp'=4] {'tp'}, dimensions={0}, use_global_device_ids=true | all-gather | bytes 7680 | tf_op jit(solution)/shard_map/all_gather | solution.py:17
  62.7 1.5 %while.39 = (s32[]{:T(128)}, f32[6,64]{1,0:T(8,128)S(1)}, f32[6,64]{1,0:T(8,128)S(1)}, f32[6,8192]{1,0:T(8,128)S(1)}, f32[4,6,64]{2,1,0:T(8,128)S(1)}, /*index=5...) while((s32[]{:T(128)}, f32[6,64]{1,0:T(8,128)S(1)}, ...), condition=%wide.region_17.18_spmd, body=%wide.region_16.17_spmd.sunk | while | flops 149765 | bytes 1391767 | solution.py:23
  64.3 1.1 copy.71
  65.4 1.0 fusion.17
  66.4 0.7 convolution_bitcast_fusion.1
  67.1 10.1 %all-gather.8 = f32[4,6,8192]{2,1,0:T(8,128)S(1)} all-gather(f32[1,6,8192]{2,1,0:T(8,128)S(1)} %convolution_bitcast_fusion.1), channel_id=4, replica_groups=mesh['groups'=2,'inst'=4,'tp'=4] {'tp'}, dimensions={0}, use_global_device_ids=true | all-gather | bytes 983040 | tf_op jit(solution)/shard_map/all_gather | solution.py:17
  77.3 0.9 copy.51
  78.3 5.2 %all-gather.7 = f32[4,6,64]{2,1,0:T(8,128)S(1)} all-gather(f32[1,6,64]{2,1,0:T(8,128)S(1)} %convolution_bitcast_fusion.3), channel_id=3, replica_groups=mesh['groups'=2,'inst'=4,'tp'=4] {'tp'}, dimensions={0}, use_global_device_ids=true | all-gather | bytes 7680 | tf_op jit(solution)/shard_map/all_gather | solution.py:17
  83.5 5.4 %all-gather.6 = f32[4,6,64]{2,1,0:T(8,128)S(1)} all-gather(f32[1,6,64]{2,1,0:T(8,128)S(1)} %bitcast.213), channel_id=2, replica_groups=mesh['groups'=2,'inst'=4,'tp'=4] {'tp'}, dimensions={0}, use_global_device_ids=true | all-gather | bytes 7680 | tf_op jit(solution)/shard_map/all_gather | solution.py:17
  88.9 1.5 %while.38 = (s32[]{:T(128)}, f32[6,64]{1,0:T(8,128)S(1)}, f32[6,64]{1,0:T(8,128)S(1)}, f32[6,8192]{1,0:T(8,128)S(1)}, f32[4,6,64]{2,1,0:T(8,128)S(1)}, /*index=5...) while((s32[]{:T(128)}, f32[6,64]{1,0:T(8,128)S(1)}, ...), condition=%wide.region_10.11_spmd, body=%wide.region_9.10_spmd.sunk | while | flops 149765 | bytes 1391767 | solution.py:23
  90.5 0.7 fusion.55
  91.2 0.6 gather_fusion
  91.8 0.7 broadcast_select_fusion.3
  92.5 0.7 gather_fusion.1
  93.2 13.5 %convolution_convert_fusion.4 = bf16[6,2048]{1,0:T(8,128)(2,1)} fusion(bf16[8192,2048]{1,0:T(8,128)(2,1)} %param.14, f32[6,8192]{1,0:T(8,128)S(1)} %get-tuple-element.359, f32[1,6,64,128]{3,2,1,0:T(8,128)S(1)} %broadcast_bitcast_fusion.4), kind=kOutput, calls=%fused_computation.36 | convolution fusion | flops 201437184 | bytes 33972224 | tf_op jit(solution)/shard_map/dot_general | solution.py:133
  106.7 13.5 %convolution_convert_fusion.5 = bf16[6,2048]{1,0:T(8,128)(2,1)} fusion(bf16[8192,2048]{1,0:T(8,128)(2,1)} %param.14, f32[6,8192]{1,0:T(8,128)S(1)} %get-tuple-element.357, f32[1,6,64,128]{3,2,1,0:T(8,128)S(1)} %broadcast_bitcast_fusion.5), kind=kOutput, calls=%fused_computation.37 | convolution fusion | flops 201437184 | bytes 33972224 | tf_op jit(solution)/shard_map/dot_general | solution.py:133
  120.6 1.8 %scatter_fusion = bf16[16,2,16,1024]{3,2,1,0:T(8,128)(2,1)S(1)} fusion(bf16[16,2,16,1024]{3,2,1,0:T(8,128)(2,1)S(1)} %get-tuple-element.407, s32[8]{0:T(128)S(1)} %fusion.57, bf16[8,2,16,1024]{3,2,1,0:T(8,128)(2,1)} %bitcast.39), kind=kCustom, calls=%fused_computation.6 | custom fusion | bytes 1572896 | tf_op jit(solution)/shard_map/scatter | solution.py:182
  122.4 0.8 scatter_fusion.1
  123.2 1.0 copy-done.1
  (101 shorter events, 6.5 us)
Async XLA Ops:
  0.6 90.6 %copy-start = (s32[4,8]{1,0:T(4,128)S(1)}, s32[4,8]{1,0:T(4,128)}, u32[]{:S(2)}) copy-start(s32[4,8]{1,0:T(4,128)} %param.19) | copy-start | bytes 388
  3.9 32.1 %copy-start.8 = (pred[4]{0:T(512)(128)(4,1)}, pred[4]{0:T(512)(128)(4,1)S(1)}, u32[]{:S(2)}) copy-start(pred[4]{0:T(512)(128)(4,1)S(1)} %fusion.53) | copy-start | bytes 16
  17.8 3.2 %copy-start.2 = (bf16[6,10240]{1,0:T(8,128)(2,1)}, bf16[6,10240]{1,0:T(8,128)(2,1)S(1)}, u32[]{:S(2)}) copy-start(bf16[6,10240]{1,0:T(8,128)(2,1)S(1)} %all_gather.49) | copy-start | bytes 368644
  20.1 2.4 %copy-start.7 = (s32[1024]{0:T(1024)}, s32[1024]{0:T(1024)S(1)}, u32[]{:S(2)}) copy-start(s32[1024]{0:T(1024)S(1)} %pad_clamp_fusion.3) | copy-start | bytes 12292
  20.7 1.8 %copy-start.5 = (s32[2,4]{1,0:T(2,128)}, s32[2,4]{1,0:T(2,128)S(1)}, u32[]{:S(2)}) copy-start(s32[2,4]{1,0:T(2,128)S(1)} %gather_fusion.4) | copy-start | bytes 100
  21.0 15.3 %copy-start.3 = (pred[16,16]{1,0:T(8,128)(4,1)}, pred[16,16]{1,0:T(8,128)(4,1)S(1)}, u32[]{:S(2)}) copy-start(pred[16,16]{1,0:T(8,128)(4,1)S(1)} %get-tuple-element.419) | copy-start | bytes 772
  21.0 27.4 %copy-start.4 = (pred[16,16]{1,0:T(8,128)(4,1)}, pred[16,16]{1,0:T(8,128)(4,1)S(1)}, u32[]{:S(2)}) copy-start(pred[16,16]{1,0:T(8,128)(4,1)S(1)} %get-tuple-element.424) | copy-start | bytes 772
  24.0 96.6 %all-to-all-start = ((bf16[4,2,2,16,1024]{4,3,2,1,0:T(8,128)(2,1)}), bf16[4,2,2,16,1024]{4,3,2,1,0:T(8,128)(2,1)}, u32[]{:S(2)}, u32[]{:S(2)}) async-start(bf16[4,2,2,16,1024]{4,3,2,1,0:T(8,128)(2,1)} %broadcast_select_fusion.2), calls=%async_computation | async-start | bytes 1048576 | tf_op jit(solution)/shard_map/all_to_all | solution.py:180
  93.2 27.0 %copy-start.10 = (pred[4]{0:T(512)(128)(4,1)S(1)}, pred[4]{0:T(512)(128)(4,1)}, u32[]{:S(2)}) copy-start(pred[4]{0:T(512)(128)(4,1)} %fusion.54) | copy-start | bytes 16
  93.2 27.2 %copy-start.6 = (s32[2,4]{1,0:T(2,128)S(1)}, s32[2,4]{1,0:T(2,128)}, u32[]{:S(2)}) copy-start(s32[2,4]{1,0:T(2,128)} %copy-done.5) | copy-start | bytes 100
  93.2 27.2 %copy-start.9 = (pred[4]{0:T(512)(128)(4,1)S(1)}, pred[4]{0:T(512)(128)(4,1)}, u32[]{:S(2)}) copy-start(pred[4]{0:T(512)(128)(4,1)} %copy-done.8) | copy-start | bytes 16
  123.2 1.0 copy-start.1
where the time goes:
time: 125 us; the launch traced here: 124 us
  blocking collectives  53.9 us (43%)
  matrix products  33.4 us (27%)
  local copies, waits for them, and re-layouts  17.9 us (14%)
  other arithmetic  12.7 us (10%)
  starting transfers between devices  5.05 us (4%)
    all_gather x6, blocking collectives, merged(): everything = jax.tree.map(lambda part: lax.all_gather(part, axis), x)  41.2 us
    dot_general x2, matrix products, project(): jnp.dot(mixed, w_out, preferred_element_type=jnp.float32)  26.9 us
    all_gather x2, blocking collectives, gather_rows(): return lax.all_gather(token_rows, 'tp', axis=1, tiled=True)  12.7 us
    all_to_all x1, starting transfers between devices, local(): lax.all_to_all(outgoing, 'inst', split_axis=0, concat_axis=0, tiled=True)  5.05 us
    unnamed x30, local copies, waits for them, and re-layouts  3.69 us
  transfers between devices with their start and end apart: 1, of which 0 were waited for; matrix products, arithmetic and copies ran while one was open for 40% of the time, Pallas kernels for 0%

commit v1 on v0

v1 whole, which is shorter than its diff:
```python
import functools
import math

import jax
import jax.numpy as jnp
from jax import lax
from jax.experimental import pallas as pl
from jax.experimental.pallas import tpu as pltpu
from jax.sharding import PartitionSpec as P

QUERY_HEADS = 64
KEY_VALUE_HEADS = 8
HEAD_SIZE = 128
NEG_LARGE = -1e30
FAR = 1 << 30
MESH = pl.DeviceIdType.MESH


def kernel(
    sizes,
    x_ref,
    aux_ref,
    moves,
    table,
    dests,
    cache_hbm,
    w_hbm,
    o1_ref,
    o2_ref,
    kv_hbm,
    full,
    cache,
    part,
    stat,
    land,
    land_stat,
    mixed,
    acc,
    wbuf,
    outgoing,
    arrived,
    cache_sem,
    w_sem,
    send_sem,
    recv_sem,
    page_send,
    page_recv,
):
    tp, inst, row_count, max_pages, move_count = sizes
    rank = lax.axis_index("tp")
    me = lax.axis_index("inst")
    rows, cw = x_ref.shape
    pages, _, extent, width = cache.shape
    spots = pages * extent
    heads_per = QUERY_HEADS // tp
    group = QUERY_HEADS // KEY_VALUE_HEADS
    hd = HEAD_SIZE
    per_rank = max_pages // tp
    chunk = wbuf.shape[1]

    load_cache = pltpu.make_async_copy(cache_hbm, cache, cache_sem.at[0])
    load_cache.start()
    for t in range(tp):
        pltpu.make_async_copy(
            w_hbm.at[pl.ds(t * chunk, chunk), :], wbuf.at[t], w_sem.at[t]
        ).start()

    barrier = pltpu.get_barrier_semaphore()
    for k in range(1, tp):
        pl.semaphore_signal(
            barrier, inc=1, device_id={"tp": lax.rem(rank + k, tp)}, device_id_type=MESH
        )
    for k in range(1, inst):
        pl.semaphore_signal(
            barrier, inc=1, device_id={"inst": lax.rem(me + k, inst)}, device_id_type=MESH
        )
    pl.semaphore_wait(barrier, tp - 1 + inst - 1)

    def exchange(phase, k, src, dst):
        return pltpu.make_async_remote_copy(
            src_ref=src,
            dst_ref=dst,
            send_sem=send_sem.at[phase, k],
            recv_sem=recv_sem.at[phase, k],
            device_id={"tp": lax.rem(rank + k, tp)},
            device_id_type=MESH,
        )

    started = []
    gathers = [exchange(0, k, x_ref, full.at[rank]) for k in range(1, tp)]
    for copy in gathers:
        copy.start()
    started += gathers
    full[rank] = x_ref[...]

    column = lax.broadcasted_iota(jnp.int32, (rows, spots), 1)
    page_id = column // extent + rank * pages
    offset = lax.rem(column, extent)
    pos = jnp.full((rows, spots), FAR, jnp.int32)
    for n in range(max_pages):
        pos = jnp.where(aux_ref[:, n : n + 1] == page_id, n * extent + offset, pos)
    target = aux_ref[:, max_pages : max_pages + 1]
    visible = pos <= target
    hit = jnp.where(pos == target, 1.0, 0.0)
    hit_t = hit.T.astype(jnp.bfloat16)
    written = jnp.dot(
        hit_t, jnp.ones((rows, hd), jnp.bfloat16), preferred_element_type=jnp.float32
    ) > 0.5
    visible_all = jnp.concatenate([visible.astype(jnp.int32)] * group, axis=0) > 0

    sources = [moves[m, 0] // row_count for m in range(move_count)]
    send_has, send_page, recv_has, recv_page = [], [], [], []
    for k in range(1, inst):
        dst = lax.rem(me + k, inst)
        src = lax.rem(me + inst - k, inst)
        out_has = jnp.int32(0)
        out_row = jnp.int32(0)
        in_has = jnp.int32(0)
        in_move = jnp.int32(0)
        for m in range(move_count):
            goes = (sources[m] == me) & (moves[m, 1] == dst)
            comes = (sources[m] == src) & (moves[m, 1] == me)
            out_has = jnp.where(goes, 1, out_has)
            out_row = jnp.where(goes, moves[m, 0] - me * row_count, out_row)
            in_has = jnp.where(comes, 1, in_has)
            in_move = jnp.where(comes, m, in_move)
        for j in range(per_rank):
            send_has.append(out_has)
            found = table[out_row, rank + tp * j] - rank * pages
            send_page.append(jnp.clip(found, 0, pages - 1))
            recv_has.append(in_has)
            recv_page.append(dests[in_move, rank + tp * j] - rank * pages)

    load_cache.wait()
    for copy in gathers:
        copy.wait_recv()

    def token_columns(c):
        return full[c // cw, :, c % cw : c % cw + hd]

    base = QUERY_HEADS * hd
    for which in range(2):
        for g in range(KEY_VALUE_HEADS):
            fresh = token_columns(base + which * width + g * hd)
            placed = jnp.dot(hit_t, fresh, preferred_element_type=jnp.float32)
            old = cache[:, which, :, g * hd : (g + 1) * hd].reshape(spots, hd)
            new = jnp.where(written, placed, old.astype(jnp.float32)).astype(jnp.bfloat16)
            cache[:, which, :, g * hd : (g + 1) * hd] = new.reshape(pages, extent, hd)

    page_copies = []
    for k in range(1, inst):
        for j in range(per_rank):
            outgoing[k - 1, j] = cache[send_page[(k - 1) * per_rank + j]]
        copy = pltpu.make_async_remote_copy(
            src_ref=outgoing.at[k - 1],
            dst_ref=arrived.at[k - 1],
            send_sem=page_send.at[k - 1],
            recv_sem=page_recv.at[k - 1],
            device_id={"inst": lax.rem(me + k, inst)},
            device_id_type=MESH,
        )
        copy.start()
        page_copies.append(copy)

    scale = 1.0 / math.sqrt(hd)
    lane = lax.broadcasted_iota(jnp.int32, (rows, 128), 1)
    stats = [jnp.zeros((rows, 128), jnp.float32) for _ in range(tp)]
    for g in range(KEY_VALUE_HEADS):
        queries = jnp.concatenate(
            [token_columns((g * group + j) * hd) for j in range(group)], axis=0
        )
        keys = cache[:, 0, :, g * hd : (g + 1) * hd].reshape(spots, hd)
        values = cache[:, 1, :, g * hd : (g + 1) * hd].reshape(spots, hd)
        scores = (
            lax.dot_general(
                queries, keys, (((1,), (1,)), ((), ())), preferred_element_type=jnp.float32
            )
            * scale
        )
        scores = jnp.where(visible_all, scores, NEG_LARGE)
        top = jnp.max(scores, axis=1, keepdims=True)
        exponent = jnp.where(visible_all, jnp.exp(scores - top), 0.0)
        total = jnp.sum(exponent, axis=1, keepdims=True)
        summed = jnp.dot(
            exponent.astype(jnp.bfloat16), values, preferred_element_type=jnp.float32
        ).astype(jnp.bfloat16)
        for j in range(group):
            h = g * group + j
            t, at = h // heads_per, h % heads_per
            take = slice(j * rows, (j + 1) * rows)
            part[t, :, at * hd : (at + 1) * hd] = summed[take]
            stats[t] = jnp.where(
                lane == at, top[take], jnp.where(lane == 64 + at, total[take], stats[t])
            )
    for t in range(tp):
        stat[t] = stats[t]

    sums = []
    for k in range(1, tp):
        peer = lax.rem(rank + k, tp)
        sums.append(
            (
                exchange(1, k, part.at[peer], land.at[k - 1]),
                exchange(2, k, stat.at[peer], land_stat.at[k - 1]),
            )
        )
    for pair in sums:
        pair[1].start()
        pair[0].start()
        started += pair
    for pair in sums:
        pair[1].wait_recv()
        pair[0].wait_recv()

    all_stats = [stat[rank]] + [land_stat[k] for k in range(tp - 1)]
    highest = functools.reduce(jnp.maximum, all_stats)
    scales = [jnp.exp(s - highest) for s in all_stats]
    whole = functools.reduce(
        jnp.add, [pltpu.roll(s, 64, 1) * f for s, f in zip(all_stats, scales)]
    )
    whole = jnp.where(whole > 0.0, whole, 1.0)
    factors = [f / whole for f in scales]
    for at in range(heads_per):
        span = slice(at * hd, (at + 1) * hd)
        merged = part[rank, :, span].astype(jnp.float32) * factors[0][:, at : at + 1]
        for k in range(tp - 1):
            merged += land[k, :, span].astype(jnp.float32) * factors[k + 1][:, at : at + 1]
        mixed[rank, :, span] = merged.astype(jnp.bfloat16)

    shares = [exchange(3, k, mixed.at[rank], mixed.at[rank]) for k in range(1, tp)]
    for copy in shares:
        copy.start()
    started += shares

    columns = wbuf.shape[2]
    tile = min(256, columns)

    def project(k):
        t = lax.rem(rank + tp - k, tp)
        pltpu.make_async_copy(
            w_hbm.at[pl.ds(0, chunk), :], wbuf.at[t], w_sem.at[t]
        ).wait()

        def step(n, carry):
            span = pl.ds(pl.multiple_of(n * tile, tile), tile)
            product = jnp.dot(
                mixed[t], wbuf[t, :, span], preferred_element_type=jnp.float32
            )
            if k == 0:
                acc[:, span] = product
            else:
                acc[:, span] += product
            return carry

        lax.fori_loop(0, columns // tile, step, 0)

    project(0)
    for k in range(1, tp):
        shares[k - 1].wait_recv()
        project(k)

    for copy in page_copies:
        copy.wait_recv()
    slots = (inst - 1) * per_rank
    for p in range(pages):
        source = jnp.int32(0)
        lands = jnp.int32(0)
        freed = jnp.int32(0)
        for i in range(slots):
            match = (recv_has[i] == 1) & (recv_page[i] == p)
            source = jnp.where(match, i, source)
            lands = jnp.where(match, 1, lands)
            freed = jnp.where((send_has[i] == 1) & (send_page[i] == p), 1, freed)
        kept = jnp.where(freed == 1, jnp.zeros((), jnp.bfloat16), cache[p])
        if slots:
            kept = jnp.where(
                lands == 1, arrived[source // per_rank, lax.rem(source, per_rank)], kept
            )
        cache[p] = kept
    store = pltpu.make_async_copy(cache, kv_hbm, cache_sem.at[1])
    store.start()
    o1_ref[...] = acc[0:row_count].astype(jnp.bfloat16)
    o2_ref[...] = acc[row_count : 2 * row_count].astype(jnp.bfloat16)
    for copy in started + page_copies:
        copy.wait_send()
    store.wait()


def local(qkv_first, qkv_second, w_out, kv_cache, lengths, page_table, moves, dest_pages):
    tp = lax.axis_size("tp")
    inst = lax.axis_size("inst")
    me = lax.axis_index("inst")
    row_count, max_pages = page_table.shape
    rows = -(-2 * row_count // 16) * 16
    spare = rows - 2 * row_count
    cw = qkv_first.shape[1]
    columns = w_out.shape[1]
    depth = QUERY_HEADS * HEAD_SIZE
    share = depth // tp
    per_rank = max_pages // tp
    mine = lax.dynamic_slice_in_dim(lengths, me * row_count, row_count)
    tokens = jnp.concatenate(
        [qkv_first, qkv_second, jnp.zeros((spare, cw), qkv_first.dtype)], axis=0
    )
    targets = jnp.concatenate([mine, mine + 1, jnp.full((spare,), -5, jnp.int32)])
    owners = jnp.concatenate(
        [page_table, page_table, jnp.full((spare, max_pages), -1, jnp.int32)], axis=0
    )
    aux = jnp.concatenate([owners, targets[:, None]], axis=1)
    sizes = (tp, inst, row_count, max_pages, moves.shape[0])
    vmem = pl.BlockSpec(memory_space=pltpu.VMEM)
    smem = pl.BlockSpec(memory_space=pltpu.SMEM)
    anywhere = pl.BlockSpec(memory_space=pl.ANY)
    page = kv_cache.shape[1:]
    bf16, f32 = jnp.bfloat16, jnp.float32
    others = max(tp - 1, 1)
    far = max(inst - 1, 1)
    dma = pltpu.SemaphoreType.DMA
    return pl.pallas_call(
        functools.partial(kernel, sizes),
        out_shape=(
            jax.ShapeDtypeStruct((row_count, columns), bf16),
            jax.ShapeDtypeStruct((row_count, columns), bf16),
            jax.ShapeDtypeStruct(kv_cache.shape, bf16),
        ),
        in_specs=[vmem, vmem, smem, smem, smem, anywhere, anywhere],
        out_specs=(vmem, vmem, anywhere),
        scratch_shapes=[
            pltpu.VMEM((tp, rows, cw), bf16),
            pltpu.VMEM(kv_cache.shape, bf16),
            pltpu.VMEM((tp, rows, share), bf16),
            pltpu.VMEM((tp, rows, 128), f32),
            pltpu.VMEM((others, rows, share), bf16),
            pltpu.VMEM((others, rows, 128), f32),
            pltpu.VMEM((tp, rows, share), bf16),
            pltpu.VMEM((rows, columns), f32),
            pltpu.VMEM((tp, share, columns), bf16),
            pltpu.VMEM((far, per_rank) + page, bf16),
            pltpu.VMEM((far, per_rank) + page, bf16),
            dma((2,)),
            dma((tp,)),
            dma((4, tp)),
            dma((4, tp)),
            dma((far,)),
            dma((far,)),
        ],
        compiler_params=pltpu.CompilerParams(
            collective_id=0, has_side_effects=True, vmem_limit_bytes=56 << 20
        ),
    )(tokens, aux, moves, page_table, dest_pages, kv_cache, w_out)


def solution(mesh):
    placed = (
        P(("groups", "inst"), "tp"),
        P(("groups", "inst"), "tp"),
        P(None, "tp"),
        P(("groups", "inst", "tp"), None, None, None),
        P("groups"),
        P(("groups", "inst"), None),
        P("groups", None),
        P("groups", None),
    )
    return jax.shard_map(
        local,
        mesh=mesh,
        in_specs=placed,
        out_specs=(
            P(("groups", "inst"), "tp"),
            P(("groups", "inst"), "tp"),
            P(("groups", "inst", "tp"), None, None, None),
        ),
        check_vma=False,
    )
```

time: 125 us -> 40.8 us (0.33)
  blocking collectives: 53.9 us -> 0 us
  matrix products: 33.4 us -> 0 us
  Pallas kernels: 0 us -> 29.4 us
  local copies, waits for them, and re-layouts: 17.9 us -> 6.56 us
  other arithmetic: 12.7 us -> 3.75 us
  starting transfers between devices: 5.05 us -> 0 us
    all_gather x8 -> x0, blocking collectives: 53.9 us -> none  [the longest x6 41.2 us: merged(): everything = jax.tree.map(lambda part: lax.all_gather(part, axis), x)]
    dot_general x14 -> x0, matrix products: 33.4 us -> none  [the longest x2 26.9 us: project(): jnp.dot(mixed, w_out, preferred_element_type=jnp.float32)]
    pallas_call x0 -> x1, Pallas kernels: none -> 29.4 us  [local(): pl.pallas_call(functools.partial(kernel, sizes), out_shape=(jax.ShapeDtyp...]
    all_to_all x1 -> x0, starting transfers between devices: 5.05 us -> none  [local(): lax.all_to_all(outgoing, 'inst', split_axis=0, concat_axis=0, tiled=True)]
    gather x7 -> x0, local copies, waits for them, and re-layouts: 4.35 us -> none  [the longest x3 1.89 us: local(): page_table[send_rows][:, rank_cols] - tp_rank * shared_pages]
    select_n x14 -> x0, other arithmetic: 3.82 us -> none  [the longest x1 1.47 us: write_tokens(): return jnp.where(page_hit[:, None, :, None], placed, paged_memory)]
    reduce_sum x5 -> x0, other arithmetic: 3.67 us -> none  [the longest x1 1.99 us: partials(): page_total = jnp.sum(exponent, axis=3).reshape(shared_pages, QUERY_HEADS)]
    concatenate x0 -> x2, other arithmetic: none -> 2.95 us  [the longest x1 1.51 us: local(): jnp.concatenate([qkv_first, qkv_second, jnp.zeros((spare, cw), qkv_first....]
  transfers between devices with their start and end apart: 1 -> 0, of which waited for: 0 -> 0; matrix products, arithmetic and copies ran while one was open for 40% -> 0% of each run, Pallas kernels for 0% -> 0%
where the time goes in v1:
time: 40.8 us; the launch traced here: 40.4 us
  Pallas kernels  29.4 us (72%)
  local copies, waits for them, and re-layouts  6.56 us (16%)
  other arithmetic  3.75 us (9%)
  between operations  0.66 us (2%)
    pallas_call x1, Pallas kernels, local(): pl.pallas_call(functools.partial(kernel, sizes), out_shape=(jax.ShapeDtyp...  29.4 us
    unnamed x4, local copies, waits for them, and re-layouts  6.39 us
    concatenate x1, other arithmetic, local(): jnp.concatenate([qkv_first, qkv_second, jnp.zeros((spare, cw), qkv_first....  1.51 us
    concatenate x1, other arithmetic, local(): aux = jnp.concatenate([owners, targets[:, None]], axis=1)  1.43 us

profile of v1, /device:TPU:0, one launch (start us, length us, event | category | flops | bytes accessed | tf_op | source)
XLA Modules:
  0.0 40.4 jit_solution(15812046827447641043)
XLA Ops:
  0.6 0.1 pad.9.clone
  0.7 0.7 %broadcast_add_fusion = (s32[6]{0:T(128)S(1)}, s32[6]{0:T(128)S(1)}) fusion(s32[24]{0:T(128)} %param.12, s32[]{:T(128)S(6)} %select_n.3), kind=kLoop, calls=%fused_computation.3 | loop fusion | flops 6 | bytes 76 | tf_op jit(solution)/shard_map/add | solution.py:305
  1.5 0.1 add_bitcast_fusion
  1.5 1.3 %copy.12.moves = s32[4,2]{1,0:T(4,128)} copy(s32[4,2]{0,1:T(2,128)} %param.14) | data formatting | bytes 64 | tf_op args[6]
  2.9 0.1 copy.11
  3.0 1.4 %pad_add_fusion.aux_ref = s32[16,9]{1,0:T(8,128)} fusion(s32[16,1]{1,0:T(8,128)S(1)} %copy.11, s32[4,8]{1,0:T(4,128)S(1)} %broadcast_in_dim.10, s32[6,8]{1,0:T(8,128)} %table.1), kind=kLoop, calls=%fused_computation.1 | loop fusion | flops 432 | bytes 960 | tf_op jit(solution)/shard_map/concatenate | solution.py:309
  4.4 1.5 %maximum_maximum_fusion.x_ref = bf16[16,2560]{1,0:T(8,128)(2,1)} fusion(bf16[6,2560]{1,0:T(8,128)(2,1)} %param.9, bf16[6,2560]{1,0:T(8,128)(2,1)} %param.8, bf16[16]{0:T(256)(128)(2,1)S(1)} %pad.9.clone), kind=kLoop, calls=%fused_computation | loop fusion | flops 245760 | bytes 143392 | tf_op jit(solution)/shard_map/concatenate | solution.py:302
  5.9 29.4 %shard_map.103 = (bf16[6,2048]{1,0:T(8,128)(2,1)}, bf16[6,2048]{1,0:T(8,128)(2,1)}, bf16[16,2,16,1024]{3,2,1,0:T(8,128)(2,1)}) custom-call(bf16[16,2560]{1,0:T(8,128)(2,1)} %maximum_maximum_fusion.x_ref, s32[16,9]{1,0:T(8,128)} %pad_add_fusion.aux_ref, s32[4,2]{1,0:T(4,128)} %copy.12.moves, s32[6,8]{1,0:T(8,128)} %table.1, s32[4,8]{1,0:T(4,128)} %dests.1, ...), custom_call_target="tpu_custom_call" | custom-call | tf_op jit(solution)/shard_map/pallas_call | solution.py:319
  35.3 1.4 %copy.16 = bf16[6,2048]{1,0:T(8,128)(2,1)} copy(bf16[6,2048]{1,0:T(8,128)(2,1)} %get-tuple-element.8) | data formatting | bytes 49152
  36.7 1.4 %copy.17 = bf16[6,2048]{1,0:T(8,128)(2,1)} copy(bf16[6,2048]{1,0:T(8,128)(2,1)} %get-tuple-element.9) | data formatting | bytes 49152
  38.0 2.3 %copy.18 = bf16[16,2,16,1024]{3,2,1,0:T(8,128)(2,1)} copy(bf16[16,2,16,1024]{3,2,1,0:T(8,128)(2,1)} %get-tuple-element.10) | data formatting | bytes 2097152
  (3 shorter events, 0.0 us)

commit v2 on v1

v2 whole, which is shorter than its diff:
```python
import functools
import math

import jax
import jax.numpy as jnp
from jax import lax
from jax.experimental import pallas as pl
from jax.experimental.pallas import tpu as pltpu
from jax.sharding import PartitionSpec as P

QUERY_HEADS = 64
KEY_VALUE_HEADS = 8
HEAD_SIZE = 128
NEG_LARGE = -1e30
FAR = 1 << 30
MESH = pl.DeviceIdType.MESH


def partner(rank, k, count):
    if count & (count - 1):
        return lax.rem(rank + k, count), lax.rem(rank + count - k, count)
    other = jnp.int32(0)
    bit = 1
    while bit < count:
        mine = (rank // bit) % 2
        other = other + bit * ((1 - mine) if (k // bit) % 2 else mine)
        bit *= 2
    return other, other


def kernel(
    sizes,
    first_hbm,
    second_hbm,
    lengths_hbm,
    moves_hbm,
    table_hbm,
    dests_hbm,
    cache_hbm,
    w_hbm,
    o1_ref,
    o2_ref,
    cache,
    first,
    second,
    table_v,
    lengths,
    moves,
    table,
    dests,
    x_ref,
    full,
    part,
    stat,
    land,
    land_stat,
    mixed,
    acc,
    wbuf,
    outgoing,
    arrived,
    small_sem,
    w_sem,
    send_sem,
    recv_sem,
    page_send,
    page_recv,
):
    tp, inst, row_count, max_pages, move_count = sizes
    rank = lax.axis_index("tp")
    me = lax.axis_index("inst")
    rows, cw = x_ref.shape
    pages, _, extent, width = cache.shape
    spots = pages * extent
    heads_per = QUERY_HEADS // tp
    group = QUERY_HEADS // KEY_VALUE_HEADS
    hd = HEAD_SIZE
    per_rank = max_pages // tp
    chunk = wbuf.shape[1]
    peers = [partner(rank, k, tp)[0] for k in range(tp)]
    froms = [partner(rank, k, tp)[1] for k in range(tp)]

    loads = [
        pltpu.make_async_copy(src, dst, small_sem.at[i])
        for i, (src, dst) in enumerate(
            [
                (first_hbm, first),
                (second_hbm, second),
                (table_hbm, table_v),
                (lengths_hbm, lengths),
                (moves_hbm, moves),
                (table_hbm, table),
                (dests_hbm, dests),
                (cache_hbm, cache),
            ]
        )
    ]
    for load in loads:
        load.start()
    barrier = pltpu.get_barrier_semaphore()
    for k in range(1, tp):
        pl.semaphore_signal(
            barrier, inc=1, device_id={"tp": lax.rem(rank + k, tp)}, device_id_type=MESH
        )
    for k in range(1, inst):
        pl.semaphore_signal(
            barrier, inc=1, device_id={"inst": lax.rem(me + k, inst)}, device_id_type=MESH
        )
    for t in range(tp):
        pltpu.make_async_copy(
            w_hbm.at[pl.ds(t * chunk, chunk), :], wbuf.at[t], w_sem.at[t]
        ).start()
    loads[0].wait()
    loads[1].wait()
    pieces = [first[...].astype(jnp.float32), second[...].astype(jnp.float32)]
    if rows > 2 * row_count:
        pieces.append(jnp.zeros((rows - 2 * row_count, cw), jnp.float32))
    tokens = jnp.concatenate(pieces, axis=0).astype(jnp.bfloat16)
    x_ref[...] = tokens
    full[rank] = tokens
    pl.semaphore_wait(barrier, tp - 1 + inst - 1)

    def exchange(phase, k, src, dst):
        return pltpu.make_async_remote_copy(
            src_ref=src,
            dst_ref=dst,
            send_sem=send_sem.at[phase, k],
            recv_sem=recv_sem.at[phase, k],
            device_id={"tp": peers[k]},
            device_id_type=MESH,
        )

    started = []
    gathers = [exchange(0, k, x_ref, full.at[rank]) for k in reversed(range(1, tp))]
    for copy in gathers:
        copy.start()
    started += gathers
    for load in loads[2:7]:
        load.wait()

    column = lax.broadcasted_iota(jnp.int32, (row_count, spots), 1)
    page_id = column // extent + rank * pages
    offset = lax.rem(column, extent)
    pos = jnp.full((row_count, spots), FAR, jnp.int32)
    for n in range(max_pages):
        pos = jnp.where(table_v[:, n : n + 1] == page_id, n * extent + offset, pos)
    spread = [pos, pos]
    if rows > 2 * row_count:
        spread.append(jnp.full((rows - 2 * row_count, spots), FAR, jnp.int32))
    pos = jnp.concatenate(spread, axis=0)
    row_id = lax.broadcasted_iota(jnp.int32, (rows, spots), 0)
    target = jnp.full((rows, spots), -5, jnp.int32)
    for r in range(row_count):
        length = lengths[me * row_count + r]
        target = jnp.where(row_id == r, length, target)
        target = jnp.where(row_id == row_count + r, length + 1, target)
    visible = pos <= target
    hit = jnp.where(pos == target, 1.0, 0.0)
    hit_t = hit.T.astype(jnp.bfloat16)
    written = jnp.dot(
        hit_t, jnp.ones((rows, hd), jnp.bfloat16), preferred_element_type=jnp.float32
    ) > 0.5
    visible_all = jnp.concatenate([visible.astype(jnp.int32)] * group, axis=0) > 0

    sources = [moves[0, m] // row_count for m in range(move_count)]
    send_has, send_page, recv_has, recv_page = [], [], [], []
    for k in range(1, inst):
        dst = lax.rem(me + k, inst)
        src = lax.rem(me + inst - k, inst)
        out_has = jnp.int32(0)
        out_row = jnp.int32(0)
        in_has = jnp.int32(0)
        in_move = jnp.int32(0)
        for m in range(move_count):
            goes = (sources[m] == me) & (moves[1, m] == dst)
            comes = (sources[m] == src) & (moves[1, m] == me)
            out_has = jnp.where(goes, 1, out_has)
            out_row = jnp.where(goes, moves[0, m] - me * row_count, out_row)
            in_has = jnp.where(comes, 1, in_has)
            in_move = jnp.where(comes, m, in_move)
        for j in range(per_rank):
            send_has.append(out_has)
            found = table[out_row, rank + tp * j] - rank * pages
            send_page.append(jnp.clip(found, 0, pages - 1))
            recv_has.append(in_has)
            recv_page.append(dests[in_move, rank + tp * j] - rank * pages)
    slots = (inst - 1) * per_rank
    plan = []
    for p in range(pages):
        source = jnp.int32(0)
        lands = jnp.int32(0)
        freed = jnp.int32(0)
        for i in range(slots):
            match = (recv_has[i] == 1) & (recv_page[i] == p)
            source = jnp.where(match, i, source)
            lands = jnp.where(match, 1, lands)
            freed = jnp.where((send_has[i] == 1) & (send_page[i] == p), 1, freed)
        plan.append((source, lands, freed))

    loads[7].wait()
    for copy in gathers:
        copy.wait_recv()

    def token_columns(c):
        at = c % cw
        if not isinstance(at, int):
            at = pl.multiple_of(at, hd)
        return full[c // cw, :, pl.ds(at, hd)]

    base = QUERY_HEADS * hd
    for which in range(2):
        for g in range(KEY_VALUE_HEADS):
            fresh = token_columns(base + which * width + g * hd)
            placed = jnp.dot(hit_t, fresh, preferred_element_type=jnp.float32)
            old = cache[:, which, :, g * hd : (g + 1) * hd].reshape(spots, hd)
            new = jnp.where(written, placed, old.astype(jnp.float32)).astype(jnp.bfloat16)
            cache[:, which, :, g * hd : (g + 1) * hd] = new.reshape(pages, extent, hd)

    page_copies = []
    for k in range(1, inst):
        for j in range(per_rank):
            outgoing[k - 1, j] = cache[send_page[(k - 1) * per_rank + j]]
        page_copies.append(
            pltpu.make_async_remote_copy(
                src_ref=outgoing.at[k - 1],
                dst_ref=arrived.at[k - 1],
                send_sem=page_send.at[k - 1],
                recv_sem=page_recv.at[k - 1],
                device_id={"inst": lax.rem(me + k, inst)},
                device_id_type=MESH,
            )
        )
    for copy in page_copies:
        copy.start()

    scale = 1.0 / math.sqrt(hd)
    lane = lax.broadcasted_iota(jnp.int32, (rows, 128), 1)

    def attend(g):
        queries = jnp.concatenate(
            [token_columns((g * group + j) * hd) for j in range(group)], axis=0
        )
        at = g * hd if isinstance(g, int) else pl.multiple_of(g * hd, hd)
        keys = cache[:, 0, :, pl.ds(at, hd)].reshape(spots, hd)
        values = cache[:, 1, :, pl.ds(at, hd)].reshape(spots, hd)
        scores = (
            lax.dot_general(
                queries, keys, (((1,), (1,)), ((), ())), preferred_element_type=jnp.float32
            )
            * scale
        )
        scores = jnp.where(visible_all, scores, NEG_LARGE)
        top = jnp.max(scores, axis=1, keepdims=True)
        exponent = jnp.where(visible_all, jnp.exp(scores - top), 0.0)
        total = jnp.sum(exponent, axis=1, keepdims=True)
        summed = jnp.dot(
            exponent.astype(jnp.bfloat16), values, preferred_element_type=jnp.float32
        ).astype(jnp.bfloat16)
        return top, total, summed

    def place(stats, at, j, top, total):
        take = slice(j * rows, (j + 1) * rows)
        stats = jnp.where(lane == at, top[take], stats)
        return jnp.where(lane == 64 + at, total[take], stats)

    sums = [
        (
            exchange(1, k, part.at[peers[k]], land.at[k - 1]),
            exchange(2, k, stat.at[peers[k]], land_stat.at[k - 1]),
        )
        for k in range(1, tp)
    ]
    for pair in sums:
        started += pair
    nothing = jnp.zeros((rows, 128), jnp.float32)
    if heads_per % group == 0:
        for k in list(reversed(range(1, tp))) + [0]:
            t = peers[k]
            stats = nothing
            for i in range(heads_per // group):
                top, total, summed = attend(t * (heads_per // group) + i)
                for j in range(group):
                    at = i * group + j
                    part[t, :, at * hd : (at + 1) * hd] = summed[j * rows : (j + 1) * rows]
                    stats = place(stats, at, j, top, total)
            stat[t] = stats
            if k:
                sums[k - 1][1].start()
                sums[k - 1][0].start()
    else:
        every = [nothing for _ in range(tp)]
        for g in range(KEY_VALUE_HEADS):
            top, total, summed = attend(g)
            for j in range(group):
                h = g * group + j
                t, at = h // heads_per, h % heads_per
                part[t, :, at * hd : (at + 1) * hd] = summed[j * rows : (j + 1) * rows]
                every[t] = place(every[t], at, j, top, total)
        for t in range(tp):
            stat[t] = every[t]
        for pair in sums:
            pair[1].start()
            pair[0].start()
    for pair in sums:
        pair[1].wait_recv()
        pair[0].wait_recv()

    all_stats = [stat[rank]] + [land_stat[k] for k in range(tp - 1)]
    highest = functools.reduce(jnp.maximum, all_stats)
    scales = [jnp.exp(s - highest) for s in all_stats]
    whole = functools.reduce(
        jnp.add, [pltpu.roll(s, 64, 1) * f for s, f in zip(all_stats, scales)]
    )
    whole = jnp.where(whole > 0.0, whole, 1.0)
    factors = [f / whole for f in scales]
    for at in range(heads_per):
        span = slice(at * hd, (at + 1) * hd)
        merged = part[rank, :, span].astype(jnp.float32) * factors[0][:, at : at + 1]
        for k in range(tp - 1):
            merged += land[k, :, span].astype(jnp.float32) * factors[k + 1][:, at : at + 1]
        mixed[rank, :, span] = merged.astype(jnp.bfloat16)

    shares = [exchange(3, k, mixed.at[rank], mixed.at[rank]) for k in range(1, tp)]
    for copy in reversed(shares):
        copy.start()
    started += shares

    columns = wbuf.shape[2]
    tile = min(256, columns)

    def project(k):
        t = froms[k]
        pltpu.make_async_copy(
            w_hbm.at[pl.ds(0, chunk), :], wbuf.at[t], w_sem.at[t]
        ).wait()

        def step(n, carry):
            span = pl.ds(pl.multiple_of(n * tile, tile), tile)
            product = jnp.dot(
                mixed[t], wbuf[t, :, span], preferred_element_type=jnp.float32
            )
            if k == 0:
                acc[:, span] = product
            else:
                acc[:, span] += product
            return carry

        lax.fori_loop(0, columns // tile, step, 0)

    def settle():
        for copy in page_copies:
            copy.wait_recv()
        for p in range(pages):
            source, lands, freed = plan[p]
            kept = jnp.where(freed == 1, jnp.zeros((), jnp.bfloat16), cache[p])
            if slots:
                kept = jnp.where(
                    lands == 1, arrived[source // per_rank, source % per_rank], kept
                )
            cache[p] = kept

    project(0)
    if tp == 1:
        settle()
    for k in range(1, tp):
        shares[k - 1].wait_recv()
        project(k)
        if k == 1:
            settle()
    o1_ref[...] = acc[0:row_count].astype(jnp.bfloat16)
    o2_ref[...] = acc[row_count : 2 * row_count].astype(jnp.bfloat16)
    for copy in started + page_copies:
        copy.wait_send()


def deliver(*refs):
    count = (len(refs) - 1) // 2
    sems = refs[-1]
    copies = [
        pltpu.make_async_copy(refs[i], refs[count + i], sems.at[i]) for i in range(count)
    ]
    for copy in copies:
        copy.start()
    for copy in copies:
        copy.wait()


def local(qkv_first, qkv_second, w_out, kv_cache, lengths, page_table, moves, dest_pages):
    tp = lax.axis_size("tp")
    inst = lax.axis_size("inst")
    row_count, max_pages = page_table.shape
    rows = -(-2 * row_count // 16) * 16
    cw = qkv_first.shape[1]
    columns = w_out.shape[1]
    share = QUERY_HEADS * HEAD_SIZE // tp
    per_rank = max_pages // tp
    sizes = (tp, inst, row_count, max_pages, moves.shape[0])
    vmem = pl.BlockSpec(memory_space=pltpu.VMEM)
    anywhere = pl.BlockSpec(memory_space=pl.ANY)
    page = kv_cache.shape[1:]
    bf16, f32, i32 = jnp.bfloat16, jnp.float32, jnp.int32
    others = max(tp - 1, 1)
    far = max(inst - 1, 1)
    dma = pltpu.SemaphoreType.DMA
    out_shapes = [(row_count, columns), (row_count, columns), kv_cache.shape]
    held = pl.pallas_call(
        functools.partial(kernel, sizes),
        out_shape=tuple(pltpu.VMEM(shape, bf16) for shape in out_shapes),
        in_specs=[anywhere] * 8,
        out_specs=(vmem, vmem, vmem),
        scratch_shapes=[
            pltpu.VMEM(qkv_first.shape, bf16),
            pltpu.VMEM(qkv_second.shape, bf16),
            pltpu.VMEM(page_table.shape, i32),
            pltpu.SMEM(lengths.shape, i32),
            pltpu.SMEM(moves.shape[::-1], i32),
            pltpu.SMEM(page_table.shape, i32),
            pltpu.SMEM(dest_pages.shape, i32),
            pltpu.VMEM((rows, cw), bf16),
            pltpu.VMEM((tp, rows, cw), bf16),
            pltpu.VMEM((tp, rows, share), bf16),
            pltpu.VMEM((tp, rows, 128), f32),
            pltpu.VMEM((others, rows, share), bf16),
            pltpu.VMEM((others, rows, 128), f32),
            pltpu.VMEM((tp, rows, share), bf16),
            pltpu.VMEM((rows, columns), f32),
            pltpu.VMEM((tp, share, columns), bf16),
            pltpu.VMEM((far, per_rank) + page, bf16),
            pltpu.VMEM((far, per_rank) + page, bf16),
            dma((8,)),
            dma((tp,)),
            dma((4, tp)),
            dma((4, tp)),
            dma((far,)),
            dma((far,)),
        ],
        compiler_params=pltpu.CompilerParams(
            collective_id=0, has_side_effects=True, vmem_limit_bytes=52 << 20
        ),
    )(
        *[
            pltpu.with_memory_space_constraint(a, pltpu.HBM)
            for a in (
                qkv_first,
                qkv_second,
                lengths,
                moves.T,
                page_table,
                dest_pages,
                kv_cache,
                w_out,
            )
        ]
    )
    return pl.pallas_call(
        deliver,
        out_shape=tuple(jax.ShapeDtypeStruct(shape, bf16) for shape in out_shapes),
        in_specs=[vmem] * 3,
        out_specs=(anywhere,) * 3,
        scratch_shapes=[dma((3,))],
        compiler_params=pltpu.CompilerParams(vmem_limit_bytes=1 << 20),
    )(*[pltpu.with_memory_space_constraint(h, pltpu.VMEM) for h in held])


def solution(mesh):
    placed = (
        P(("groups", "inst"), "tp"),
        P(("groups", "inst"), "tp"),
        P(None, "tp"),
        P(("groups", "inst", "tp"), None, None, None),
        P("groups"),
        P(("groups", "inst"), None),
        P("groups", None),
        P("groups", None),
    )
    return jax.shard_map(
        local,
        mesh=mesh,
        in_specs=placed,
        out_specs=(
            P(("groups", "inst"), "tp"),
            P(("groups", "inst"), "tp"),
            P(("groups", "inst", "tp"), None, None, None),
        ),
        check_vma=False,
    )
```

time: 40.8 us -> 27.4 us (0.67)
  local copies, waits for them, and re-layouts: 6.56 us -> 0 us
  other arithmetic: 3.75 us -> 0 us
  Pallas kernels: 29.4 us -> 26.6 us
    unnamed x4 -> x0, local copies, waits for them, and re-layouts: 6.39 us -> none
    concatenate x2 -> x0, other arithmetic: 2.95 us -> none  [the longest x1 1.51 us: local(): jnp.concatenate([qkv_first, qkv_second, jnp.zeros((spare, cw), qkv_first....]
    pallas_call x1 -> x2, Pallas kernels: 29.4 us -> 26.6 us  [the longest x1 25.6 us: local(): pl.pallas_call(functools.partial(kernel, sizes), out_shape=tuple((pltpu.V...]
    add x1 -> x0, other arithmetic: 0.73 us -> none  [local(): mine + 1]
where the time goes in v2:
time: 27.4 us; the launch traced here: 27.2 us
  Pallas kernels  26.6 us (97%)
  between operations  0.64 us (2%)
    pallas_call x1, Pallas kernels, local(): pl.pallas_call(functools.partial(kernel, sizes), out_shape=tuple((pltpu.V...  25.6 us
    pallas_call x1, Pallas kernels, local(): pl.pallas_call(deliver, out_shape=tuple((jax.ShapeDtypeStruct(shape, bf16...  1.02 us

profile of v2, /device:TPU:0, one launch (start us, length us, event | category | flops | bytes accessed | tf_op | source)
XLA Modules:
  0.0 27.2 jit_solution(1779930595076208286)
XLA Ops:
  0.6 25.6 %shard_map.103 = (bf16[6,2048]{1,0:T(8,128)(2,1)S(1)}, bf16[6,2048]{1,0:T(8,128)(2,1)S(1)}, bf16[16,2,16,1024]{3,2,1,0:T(8,128)(2,1)S(1)}) custom-call(bf16[6,2560]{1,0:T(8,128)(2,1)} %first_hbm.1, bf16[6,2560]{1,0:T(8,128)(2,1)} %second_hbm.1, s32[24]{0:T(128)} %lengths_hbm.1, s32[2,4]{1,0:T(2,128)} %bitcast.1, s32[6,8]{1,0:T(8,128)} %table_hbm.1, ...), custom_call_target="tpu_custom_call" | custom-call | tf_op jit(solution)/shard_map/pallas_call | solution.py:406
  26.2 1.0 %shard_map.104 = (bf16[6,2048]{1,0:T(8,128)(2,1)}, bf16[6,2048]{1,0:T(8,128)(2,1)}, bf16[16,2,16,1024]{3,2,1,0:T(8,128)(2,1)}) custom-call(bf16[6,2048]{1,0:T(8,128)(2,1)S(1)} %get-tuple-element.6.refs_0_, bf16[6,2048]{1,0:T(8,128)(2,1)S(1)} %get-tuple-element.7.refs_1_, bf16[16,2,16,1024]{3,2,1,0:T(8,128)(2,1)S(1)} %get-tuple-element.8.refs_2_), custom_call_target="tpu_custom_call" | custom-call | tf_op jit(solution)/shard_map/pallas_call | solution.py:455

commit v3 on v2

--- a/solution.py
+++ b/solution.py
@@ -130,11 +130,34 @@
             device_id_type=MESH,
         )
 
+    relayed = tp >= 4 and tp & (tp - 1) == 0
     started = []
-    gathers = [exchange(0, k, x_ref, full.at[rank]) for k in reversed(range(1, tp))]
-    for copy in gathers:
-        copy.start()
-    started += gathers
+
+    def spread_out(phase, src, held):
+        copies = {}
+        order = list(range(2, tp)) + [1]
+        for k in order:
+            if relayed and k > 1 and k % 2:
+                copies[k] = pltpu.make_async_remote_copy(
+                    src_ref=held.at[froms[k - 1]],
+                    dst_ref=held.at[froms[k - 1]],
+                    send_sem=send_sem.at[phase, k],
+                    recv_sem=recv_sem.at[phase, k],
+                    device_id={"tp": peers[1]},
+                    device_id_type=MESH,
+                )
+            else:
+                copies[k] = exchange(phase, k, src, held.at[rank])
+                copies[k].start()
+            started.append(copies[k])
+        return copies
+
+    def arrive(copies, k):
+        copies[k].wait_recv()
+        if relayed and k > 1 and k % 2 == 0:
+            copies[k + 1].start()
+
+    gathers = spread_out(0, x_ref, full)
     for load in loads[2:7]:
         load.wait()
 
@@ -198,8 +221,8 @@
         plan.append((source, lands, freed))
 
     loads[7].wait()
-    for copy in gathers:
-        copy.wait_recv()
+    for k in [*range(2, tp, 2), 1, *range(3, tp, 2)] if relayed else range(1, tp):
+        arrive(gathers, k)
 
     def token_columns(c):
         at = c % cw
@@ -320,13 +343,10 @@
             merged += land[k, :, span].astype(jnp.float32) * factors[k + 1][:, at : at + 1]
         mixed[rank, :, span] = merged.astype(jnp.bfloat16)
 
-    shares = [exchange(3, k, mixed.at[rank], mixed.at[rank]) for k in range(1, tp)]
-    for copy in reversed(shares):
-        copy.start()
-    started += shares
+    shares = spread_out(3, mixed.at[rank], mixed)
 
     columns = wbuf.shape[2]
-    tile = min(256, columns)
+    tile = columns
 
     def project(k):
         t = froms[k]
@@ -360,13 +380,10 @@
             cache[p] = kept
 
     project(0)
-    if tp == 1:
-        settle()
     for k in range(1, tp):
-        shares[k - 1].wait_recv()
+        arrive(shares, k)
         project(k)
-        if k == 1:
-            settle()
+    settle()
     o1_ref[...] = acc[0:row_count].astype(jnp.bfloat16)
     o2_ref[...] = acc[row_count : 2 * row_count].astype(jnp.bfloat16)
     for copy in started + page_copies:

time: 27.4 us -> 24.1 us (0.88)
  Pallas kernels: 26.6 us -> 23.3 us
    pallas_call x1, Pallas kernels: 25.6 us -> 22.3 us  [local(): pl.pallas_call(functools.partial(kernel, sizes), out_shape=tuple((pltpu.V...]
where the time goes in v3:
time: 24.1 us; the launch traced here: 23.9 us
  Pallas kernels  23.3 us (97%)
  between operations  0.64 us (3%)
    pallas_call x1, Pallas kernels, local(): pl.pallas_call(functools.partial(kernel, sizes), out_shape=tuple((pltpu.V...  22.3 us
    pallas_call x1, Pallas kernels, local(): pl.pallas_call(deliver, out_shape=tuple((jax.ShapeDtypeStruct(shape, bf16...  1.02 us

profile of v3, /device:TPU:0, one launch (start us, length us, event | category | flops | bytes accessed | tf_op | source)
XLA Modules:
  0.0 23.9 jit_solution(12427628774793904612)
XLA Ops:
  0.6 22.3 %shard_map.103 = (bf16[6,2048]{1,0:T(8,128)(2,1)S(1)}, bf16[6,2048]{1,0:T(8,128)(2,1)S(1)}, bf16[16,2,16,1024]{3,2,1,0:T(8,128)(2,1)S(1)}) custom-call(bf16[6,2560]{1,0:T(8,128)(2,1)} %first_hbm.1, bf16[6,2560]{1,0:T(8,128)(2,1)} %second_hbm.1, s32[24]{0:T(128)} %lengths_hbm.1, s32[2,4]{1,0:T(2,128)} %bitcast.1, s32[6,8]{1,0:T(8,128)} %table_hbm.1, ...), custom_call_target="tpu_custom_call" | custom-call | tf_op jit(solution)/shard_map/pallas_call | solution.py:423
  22.9 1.0 %shard_map.104 = (bf16[6,2048]{1,0:T(8,128)(2,1)}, bf16[6,2048]{1,0:T(8,128)(2,1)}, bf16[16,2,16,1024]{3,2,1,0:T(8,128)(2,1)}) custom-call(bf16[6,2048]{1,0:T(8,128)(2,1)S(1)} %get-tuple-element.6.refs_0_, bf16[6,2048]{1,0:T(8,128)(2,1)S(1)} %get-tuple-element.7.refs_1_, bf16[16,2,16,1024]{3,2,1,0:T(8,128)(2,1)S(1)} %get-tuple-element.8.refs_2_), custom_call_target="tpu_custom_call" | custom-call | tf_op jit(solution)/shard_map/pallas_call | solution.py:472

commit v4 on v3

--- a/solution.py
+++ b/solution.py
@@ -381,9 +381,12 @@
 
     project(0)
     for k in range(1, tp):
+        if k == tp - 1:
+            settle()
         arrive(shares, k)
         project(k)
-    settle()
+    if tp == 1:
+        settle()
     o1_ref[...] = acc[0:row_count].astype(jnp.bfloat16)
     o2_ref[...] = acc[row_count : 2 * row_count].astype(jnp.bfloat16)
     for copy in started + page_copies:

time: 24.1 us -> 24.1 us (level)
  no operation moved by 1% of the time
where the time goes in v4:
time: 24.1 us; the launch traced here: 24 us
  Pallas kernels  23.3 us (97%)
  between operations  0.64 us (3%)
    pallas_call x1, Pallas kernels, local(): pl.pallas_call(functools.partial(kernel, sizes), out_shape=tuple((pltpu.V...  22.3 us
    pallas_call x1, Pallas kernels, local(): pl.pallas_call(deliver, out_shape=tuple((jax.ShapeDtypeStruct(shape, bf16...  1.02 us

profile of v4, /device:TPU:0, one launch (start us, length us, event | category | flops | bytes accessed | tf_op | source)
XLA Modules:
  0.0 24.0 jit_solution(3594895506994541325)
XLA Ops:
  0.6 22.3 %shard_map.103 = (bf16[6,2048]{1,0:T(8,128)(2,1)S(1)}, bf16[6,2048]{1,0:T(8,128)(2,1)S(1)}, bf16[16,2,16,1024]{3,2,1,0:T(8,128)(2,1)S(1)}) custom-call(bf16[6,2560]{1,0:T(8,128)(2,1)} %first_hbm.1, bf16[6,2560]{1,0:T(8,128)(2,1)} %second_hbm.1, s32[24]{0:T(128)} %lengths_hbm.1, s32[2,4]{1,0:T(2,128)} %bitcast.1, s32[6,8]{1,0:T(8,128)} %table_hbm.1, ...), custom_call_target="tpu_custom_call" | custom-call | tf_op jit(solution)/shard_map/pallas_call | solution.py:426
  22.9 1.0 %shard_map.104 = (bf16[6,2048]{1,0:T(8,128)(2,1)}, bf16[6,2048]{1,0:T(8,128)(2,1)}, bf16[16,2,16,1024]{3,2,1,0:T(8,128)(2,1)}) custom-call(bf16[6,2048]{1,0:T(8,128)(2,1)S(1)} %get-tuple-element.6.refs_0_, bf16[6,2048]{1,0:T(8,128)(2,1)S(1)} %get-tuple-element.7.refs_1_, bf16[16,2,16,1024]{3,2,1,0:T(8,128)(2,1)S(1)} %get-tuple-element.8.refs_2_), custom_call_target="tpu_custom_call" | custom-call | tf_op jit(solution)/shard_map/pallas_call | solution.py:475
